TPU v7x, 32 devices: a whole 2x2x4 slice. The times are simulated.
32 devices in a mesh: grp: 2 (over x), wide: 16 (over z, y, core).
Axes of the slice: x: 2, y: 2, z: 4, core: 2. Of those that a mesh axis runs over, the one named last changes fastest.
Arguments:
- queries: bfloat16 [256, 4096], P(('grp', 'wide')), parts along dimension 0, may hold values from -8 to 8
- draft_keys: bfloat16 [256, 512], P(('grp', 'wide')), parts along dimension 0, may hold values from -8 to 8
- draft_values: bfloat16 [256, 512], P(('grp', 'wide')), parts along dimension 0, may hold values from -24 to 24
- cache_keys: bfloat16 [262144, 128], P(('grp', 'wide')), parts along dimension 0, may hold values from -8 to 8
- cache_values: bfloat16 [262144, 128], P(('grp', 'wide')), parts along dimension 0, may hold values from -24 to 24
- block_owner: int32 [32], P('grp'), parts along dimension 0, may hold values from 0 to 15, each once
- block_lengths: int32 [32], P('grp'), parts along dimension 0, may hold values from 1024 to 8192, as said below
- draft_mask: int32 [4, 64, 64], P('grp'), parts along dimension 0, may hold values from 0 to 1, as said below
- out_weight: bfloat16 [4096, 8192], P(None, 'wide'), may hold values from -1 to 1
- norm_gain: float32 [8192], replicated, may hold values from 0.25 to 1.75
- gate_weight: bfloat16 [8192, 14336], P(None, 'wide'), may hold values from -0.0625 to 0.0625
- up_weight: bfloat16 [8192, 14336], P(None, 'wide'), may hold values from -0.0625 to 0.0625
Outputs:
- projected: bfloat16 [256, 8192], P('grp', 'wide'), parts along dimension 0
- hidden: bfloat16 [256, 14336], P('grp', 'wide'), parts along dimension 0
There are 2 independent parts, one for each index of `grp`. A program takes and returns all parts, laid end to end along the dimension named above; an argument that names none is the same for every part. Nothing has to cross between parts.
Inputs may be any that keep to these rules, and one draw needn't show every extreme that they name: `block_owner`: each device holds exactly one block. `block_lengths`: at most 8192 rows a block, and some block has exactly 8192 rows. In each sequence row 0 is the root of a tree in which every other row's parent lies 1 to 4 rows before it; draft_mask[s, i, t] is 1 exactly when t is i or an ancestor of i.
All inputs are finite; a program needn't handle non-finite values.
Results may differ from a plain program's by a relative error of at most 0.02.
Values may be sent and summed in bfloat16 or wider, within the bound.
A program may use at most 128 MiB of HBM per device.

v0:
```python
import math

import jax
import jax.numpy as jnp
from jax import lax
from jax.sharding import PartitionSpec as P

very_low = -1e30
epsilon = 1e-05


def block_update(state, query_rows, block_keys, block_values, valid, scale):
    running, total, weighted = state
    scores = (
        jnp.einsum("igc,kc->igk", query_rows, block_keys, preferred_element_type=jnp.float32)
        * scale
    )
    scores = jnp.where(valid, scores, very_low)
    newest = jnp.maximum(running, jnp.max(scores, axis=-1))
    factor = jnp.exp(running - newest)
    weights = jnp.where(valid, jnp.exp(scores - newest[..., None]), 0.0)
    total = total * factor + jnp.sum(weights, axis=-1)
    weighted = weighted * factor[..., None] + jnp.einsum(
        "igk,kc->igc",
        weights.astype(jnp.bfloat16),
        block_values,
        preferred_element_type=jnp.float32,
    )
    return (newest, total, weighted)


def attend(query_rows, keys, values, length, own_keys, own_values, own_valid):
    block_size = min(512, keys.shape[0])
    scale = 1.0 / math.sqrt(query_rows.shape[2])
    rows_count = query_rows.shape[0]
    heads = query_rows.shape[1]
    state = (
        jnp.full((rows_count, heads), very_low, jnp.float32),
        jnp.zeros((rows_count, heads), jnp.float32),
        jnp.zeros((rows_count, heads, query_rows.shape[2]), jnp.float32),
    )
    offsets = jnp.arange(block_size, dtype=jnp.int32)

    def advance(number, carry):
        begin = (number * block_size).astype(jnp.int32)
        block_keys = lax.dynamic_slice_in_dim(keys, begin, block_size, 0)
        block_values = lax.dynamic_slice_in_dim(values, begin, block_size, 0)
        valid = (begin + offsets < length)[None, None, :]
        return block_update(carry, query_rows, block_keys, block_values, valid, scale)

    count = (length + block_size - 1) // block_size
    state = lax.fori_loop(jnp.int32(0), count, advance, state)
    return block_update(state, query_rows, own_keys, own_values, own_valid[:, None, :], scale)


def per_device(
    queries,
    draft_keys,
    draft_values,
    cache_keys,
    cache_values,
    block_owner,
    block_lengths,
    draft_mask,
    out_weight,
    norm_gain,
    gate_weight,
    up_weight,
):
    devices = lax.axis_size("wide")
    own_index = lax.axis_index("wide")
    head_size = cache_keys.shape[1]
    key_heads = draft_keys.shape[1] // head_size
    group_width = queries.shape[1] // key_heads
    group = group_width // head_size
    sequences = draft_mask.shape[0]
    draft_rows = draft_mask.shape[1]
    all_rows = sequences * draft_rows
    local_rows = queries.shape[0]
    heads_all = key_heads * group
    blocks_per_pair = devices // (sequences * key_heads)
    device_ids = jnp.arange(devices, dtype=jnp.int32)
    owned = (block_owner[None, :] == device_ids[:, None]).astype(jnp.int32)
    device_block = jnp.sum(owned * device_ids[None, :], axis=1)
    device_pair = device_block // blocks_per_pair
    device_sequence = device_pair // key_heads
    device_head = device_pair % key_heads
    device_length = jnp.sum(owned * block_lengths[None, :], axis=1)
    picker = (device_ids == own_index).astype(jnp.int32)
    own_block = jnp.sum(picker * device_block)
    own_sequence = jnp.sum(picker * device_sequence)
    own_head = jnp.sum(picker * device_head)
    own_length = jnp.sum(picker * device_length)
    is_last = own_block % blocks_per_pair == blocks_per_pair - 1
    row_start = own_sequence * draft_rows
    head_numbers = jnp.arange(key_heads, dtype=jnp.int32)
    every_query, every_key, every_value = (
        lax.all_gather(queries, "wide", axis=0, tiled=True),
        lax.all_gather(draft_keys, "wide", axis=0, tiled=True),
        lax.all_gather(draft_values, "wide", axis=0, tiled=True),
    )
    query_columns = own_head * group_width
    key_columns = own_head * head_size
    pair_queries = lax.dynamic_slice_in_dim(
        lax.dynamic_slice_in_dim(every_query, row_start, draft_rows, 0),
        query_columns,
        group_width,
        1,
    )
    pair_keys = lax.dynamic_slice_in_dim(
        lax.dynamic_slice_in_dim(every_key, row_start, draft_rows, 0), key_columns, head_size, 1
    )
    pair_values = lax.dynamic_slice_in_dim(
        lax.dynamic_slice_in_dim(every_value, row_start, draft_rows, 0), key_columns, head_size, 1
    )
    own_head = jnp.sum(picker * device_head)
    query_rows = pair_queries.reshape(draft_rows, group, head_size)
    own_valid = (
        lax.dynamic_index_in_dim(draft_mask, own_sequence, 0, keepdims=False) > 0
    ) & is_last
    running, total, weighted = attend(
        query_rows, cache_keys, cache_values, own_length, pair_keys, pair_values, own_valid
    )
    block_output = (weighted / total[..., None]).astype(jnp.bfloat16)
    slot_peak = lax.dynamic_update_slice(
        jnp.full((all_rows, group), very_low, jnp.float32), running, (row_start, jnp.int32(0))
    ).reshape(devices, local_rows, group)
    slot_total = lax.dynamic_update_slice(
        jnp.zeros((all_rows, group), jnp.float32), total, (row_start, jnp.int32(0))
    ).reshape(devices, local_rows, group)
    slot_output = lax.dynamic_update_slice(
        jnp.zeros((all_rows, group, head_size), jnp.bfloat16),
        block_output,
        (row_start, jnp.int32(0), jnp.int32(0)),
    ).reshape(devices, local_rows, group, head_size)
    back_peak, back_total = (
        lax.all_to_all(slot_peak, "wide", split_axis=0, concat_axis=0, tiled=True),
        lax.all_to_all(slot_total, "wide", split_axis=0, concat_axis=0, tiled=True),
    )
    back_output = lax.all_to_all(slot_output, "wide", split_axis=0, concat_axis=0, tiled=True)
    member = device_head[:, None] == head_numbers[None, :]
    spread = jnp.where(member[:, None, :, None], back_peak[:, :, None, :], very_low)
    highest = jnp.max(spread, axis=0)
    mixing = jnp.exp(spread - highest[None]) * back_total[:, :, None, :]
    row_total = jnp.sum(mixing, axis=0)
    row_weighted = jnp.einsum(
        "srgj,srjc->rgjc", mixing, back_output.astype(jnp.float32), precision=lax.Precision.HIGHEST
    )
    attended_rows = (
        (row_weighted / row_total[..., None])
        .astype(jnp.bfloat16)
        .reshape(local_rows, heads_all * head_size)
    )
    combined = jnp.dot(
        lax.all_gather(attended_rows, "wide", axis=0, tiled=True),
        out_weight,
        preferred_element_type=jnp.float32,
    )
    projected = combined.astype(jnp.bfloat16)
    columns = projected.shape[1]
    branch = lax.optimization_barrier(projected).astype(jnp.float32)
    squares = lax.psum(jnp.sum(branch * branch, axis=1), "wide")
    inverse = lax.rsqrt(squares / (columns * devices) + epsilon)
    gain_part = lax.dynamic_slice_in_dim(norm_gain, own_index * columns, columns, 0)
    normed = (branch * inverse[:, None] * gain_part[None, :]).astype(jnp.bfloat16)
    piece = lax.all_gather(normed, "wide", axis=1, tiled=True)
    gate = jnp.dot(piece, gate_weight, preferred_element_type=jnp.float32)
    upward = jnp.dot(piece, up_weight, preferred_element_type=jnp.float32)
    hidden = (jax.nn.silu(gate) * upward).astype(jnp.bfloat16)
    return (projected, hidden)


def solution(mesh):
    placed = (
        P(("grp", "wide"), None),
        P(("grp", "wide"), None),
        P(("grp", "wide"), None),
        P(("grp", "wide"), None),
        P(("grp", "wide"), None),
        P("grp"),
        P("grp"),
        P("grp", None, None),
        P(None, "wide"),
        P(),
        P(None, "wide"),
        P(None, "wide"),
    )
    return jax.shard_map(
        per_device,
        mesh=mesh,
        in_specs=placed,
        out_specs=(P("grp", "wide"), P("grp", "wide")),
        check_vma=False,
    )
```

profile of v0, /device:TPU:0, one launch (start us, length us, event | category | flops | bytes accessed | tf_op | source)
XLA Modules:
  0.0 299.6 jit_solution(8862913507777741700)
XLA Ops:
  7.9 0.8 select_reduce_fusion.2
  8.7 0.8 select_reduce_fusion.4
  16.7 23.9 %all_gather.16 = bf16[128,512]{1,0:T(8,128)(2,1)S(1)} all-gather(bf16[8,512]{1,0:T(8,128)(2,1)} %param.15), channel_id=1, replica_groups=mesh['grp'=2,'wide'=16] {'wide'}, dimensions={0}, use_global_device_ids=true | all-gather | bytes 139264 | tf_op jit(solution)/shard_map/all_gather | solution.py:99
  40.6 0.8 fusion.41
  41.4 9.5 %all-gather.4.cloned.1.call-done = bf16[128,4096]{1,0:T(8,128)(2,1)} async-done(((bf16[8,4096]{1,0:T(8,128)(2,1)}), bf16[128,4096]{1,0:T(8,128)(2,1)}) %all-gather.4.cloned.1.call-update) | async-done | bytes 1048592 | tf_op jit(solution)/shard_map/all_gather | solution.py:98
  50.9 1.0 dynamic-slice_bitcast_fusion.1
  52.5 15.4 %while.15 = (s32[]{:T(128)}, f32[64,8]{0,1:T(8,128)S(1)}, f32[64,8]{0,1:T(8,128)S(1)}, f32[64,8,128]{2,1,0:T(8,128)S(1)}, s32[]{:T(128)}, /*index=5*/s32[]{:T(12...) while((s32[]{:T(128)}, f32[64,8]{0,1:T(8,128)S(1)}, ...), condition=%wide.region_8.9_spmd.clone, body=%wide.region_5.8_spmd.clone.sunk | while | flops 136185856 | bytes 4099771 | solution.py:52
  53.3 1.3 fusion.69
  55.0 1.3 convolution_add_fusion.3
  57.1 1.3 fusion.69
  58.9 1.3 convolution_add_fusion.3
  60.2 0.7 fusion.68
  60.9 1.3 fusion.69
  62.7 1.3 convolution_add_fusion.3
  64.8 1.3 fusion.69
  66.5 1.3 convolution_add_fusion.3
  69.2 48.1 %all-to-all-start.2 = ((f32[16,8,8]{1,2,0:T(8,128)}), f32[16,8,8]{1,2,0:T(8,128)S(1)}, u32[]{:S(2)}, u32[]{:S(2)}) async-start(f32[16,8,8]{1,2,0:T(8,128)} %copy.68), calls=%async_computation.2 | async-start | bytes 131072 | tf_op jit(solution)/shard_map/all_to_all | solution.py:138
  117.4 22.1 %all_gather.17 = bf16[128,512]{1,0:T(8,128)(2,1)S(1)} all-gather(bf16[8,512]{1,0:T(8,128)(2,1)S(1)} %copy-done.2), channel_id=1, replica_groups=mesh['grp'=2,'wide'=16] {'wide'}, dimensions={0}, use_global_device_ids=true | all-gather | bytes 139264 | tf_op jit(solution)/shard_map/all_gather | solution.py:100
  140.6 3.5 %all-to-all-start.1 = ((f32[16,8,8]{1,2,0:T(8,128)}), f32[16,8,8]{1,2,0:T(8,128)S(1)}, u32[]{:S(2)}, u32[]{:S(2)}) async-start(f32[16,8,8]{1,2,0:T(8,128)} %copy.66), calls=%async_computation.1 | async-start | bytes 131072 | tf_op jit(solution)/shard_map/all_to_all | solution.py:137
  144.1 0.7 broadcast_in_dim.96
  144.8 0.9 fusion.18
  145.8 5.2 %all-to-all-done.1 = f32[16,8,8]{1,2,0:T(8,128)S(1)} async-done(((f32[16,8,8]{1,2,0:T(8,128)}), f32[16,8,8]{1,2,0:T(8,128)S(1)}, u32[]{:S(2)}, u32[]{:S(2)}) %all-to-all-start.1) | async-done | bytes 4128 | tf_op jit(solution)/shard_map/all_to_all | solution.py:137
  151.0 3.5 %all-to-all-start = ((bf16[16,8,8,128]{3,2,1,0:T(8,128)(2,1)}), bf16[16,8,8,128]{3,2,1,0:T(8,128)(2,1)S(1)}, u32[]{:S(2)}, u32[]{:S(2)}) async-start(bf16[16,8,8,128]{3,2,1,0:T(8,128)(2,1)} %bitcast.3), calls=%async_computation | async-start | bytes 524288 | tf_op jit(solution)/shard_map/all_to_all | solution.py:140
  155.2 9.3 %all-to-all-done = bf16[16,8,8,128]{3,2,1,0:T(8,128)(2,1)S(1)} async-done(((bf16[16,8,8,128]{3,2,1,0:T(8,128)(2,1)}), bf16[16,8,8,128]{3,2,1,0:T(8,128)(2,1)S(1)}, u32[]{:S(2)}, u32[]{:S(2)}) %all-to-all-start) | async-done | bytes 262176 | tf_op jit(solution)/shard_map/all_to_all | solution.py:140
  165.8 0.8 dynamic_slice.29
  166.6 35.7 %all-gather.6.cloned.1.call-done = bf16[128,4096]{1,0:T(8,128)(2,1)} async-done(((bf16[8,4096]{1,0:T(8,128)(2,1)}), bf16[128,4096]{1,0:T(8,128)(2,1)}) %all-gather.6.cloned.1.call-update) | async-done | bytes 1048592 | tf_op jit(solution)/shard_map/all_gather | solution.py:155
  202.3 3.2 %convolution_convert_fusion = bf16[128,512]{1,0:T(8,128)(2,1)S(1)} fusion(bf16[128,4096]{1,0:T(8,128)(2,1)} %all-gather.6.cloned.1.call-done, bf16[4096,512]{1,0:T(8,128)(2,1)} %param.22), kind=kOutput, calls=%fused_computation.27 | convolution fusion | flops 536936448 | bytes 5373952 | tf_op jit(solution)/shard_map/dot_general | solution.py:154
  205.6 31.6 %psum.7 = f32[128]{0:T(128)S(1)} all-reduce(f32[128]{0:T(128)S(1)} %fusion.21), channel_id=1, replica_groups=mesh['grp'=2,'wide'=16] {'wide'}, use_global_device_ids=true, to_apply=%region_15.16 | all-reduce | flops 128 | bytes 1024 | tf_op jit(solution)/shard_map/psum | solution.py:162
  237.2 0.8 fusion.23
  238.0 38.4 %all-gather.8.cloned.1.call-done = bf16[128,8192]{1,0:T(8,128)(2,1)} async-done(((bf16[128,512]{1,0:T(8,128)(2,1)}), bf16[128,8192]{1,0:T(8,128)(2,1)}) %all-gather.8.cloned.1.call-update) | async-done | bytes 2097168 | tf_op jit(solution)/shard_map/all_gather | solution.py:166
  276.5 8.3 %fusion.50 = f32[128,896]{1,0:T(8,128)S(1)} fusion(bf16[128,8192]{1,0:T(8,128)(2,1)} %all-gather.8.cloned.1.call-done, bf16[8192,896]{1,0:T(8,128)(2,1)} %param.24), kind=kOutput, calls=%fused_computation.90 | convolution fusion | flops 1879048192 | bytes 17235968 | tf_op jit(solution)/shard_map/dot_general | solution.py:167
  284.8 8.3 %fusion.14 = bf16[128,896]{1,0:T(8,128)(2,1)} fusion(bf16[128,8192]{1,0:T(8,128)(2,1)S(1)} %copy-done, bf16[8192,896]{1,0:T(8,128)(2,1)} %param.25, f32[128,896]{1,0:T(8,128)S(1)} %fusion.50), kind=kOutput, calls=%fused_computation.20 | convolution fusion | flops 1879736320 | bytes 17465344 | tf_op jit(solution)/shard_map/dot_general | solution.py:168
  (69 shorter events, 10.3 us)
Async XLA Ops:
  7.2 43.8 %all-gather.4.cloned.1.call-start = ((), (), s32[]{:S(2)}) async-start(), calls=%async_computation.3 | async-start | bytes 1114112 | tf_op jit(solution)/shard_map/all_gather | solution.py:98
  52.5 64.9 %copy-start.2 = (bf16[8,512]{1,0:T(8,128)(2,1)S(1)}, bf16[8,512]{1,0:T(8,128)(2,1)}, u32[]{:S(2)}) copy-start(bf16[8,512]{1,0:T(8,128)(2,1)} %param.16) | copy-start | bytes 24580
  69.2 71.4 %all-to-all-start.2 = ((f32[16,8,8]{1,2,0:T(8,128)}), f32[16,8,8]{1,2,0:T(8,128)S(1)}, u32[]{:S(2)}, u32[]{:S(2)}) async-start(f32[16,8,8]{1,2,0:T(8,128)} %copy.68), calls=%async_computation.2 | async-start | bytes 131072 | tf_op jit(solution)/shard_map/all_to_all | solution.py:138
  140.6 10.4 %all-to-all-start.1 = ((f32[16,8,8]{1,2,0:T(8,128)}), f32[16,8,8]{1,2,0:T(8,128)S(1)}, u32[]{:S(2)}, u32[]{:S(2)}) async-start(f32[16,8,8]{1,2,0:T(8,128)} %copy.66), calls=%async_computation.1 | async-start | bytes 131072 | tf_op jit(solution)/shard_map/all_to_all | solution.py:137
  151.0 13.5 %all-to-all-start = ((bf16[16,8,8,128]{3,2,1,0:T(8,128)(2,1)}), bf16[16,8,8,128]{3,2,1,0:T(8,128)(2,1)S(1)}, u32[]{:S(2)}, u32[]{:S(2)}) async-start(bf16[16,8,8,128]{3,2,1,0:T(8,128)(2,1)} %bitcast.3), calls=%async_computation | async-start | bytes 524288 | tf_op jit(solution)/shard_map/all_to_all | solution.py:140
  154.5 47.8 %all-gather.6.cloned.1.call-start = ((), (), s32[]{:S(2)}) async-start(), calls=%async_computation.4 | async-start | bytes 1114112 | tf_op jit(solution)/shard_map/all_gather | solution.py:155
  165.7 110.7 %all-gather.8.cloned.1.call-start = ((), (), s32[]{:S(2)}) async-start(), calls=%async_computation.5 | async-start | bytes 2228224 | tf_op jit(solution)/shard_map/all_gather | solution.py:166
  205.5 79.3 %copy-start.1 = (bf16[128,512]{1,0:T(8,128)(2,1)}, bf16[128,512]{1,0:T(8,128)(2,1)S(1)}, u32[]{:S(2)}) copy-start(bf16[128,512]{1,0:T(8,128)(2,1)S(1)} %convolution_convert_fusion) | copy-start | bytes 393220
  276.5 8.3 %copy-start = (bf16[128,8192]{1,0:T(8,128)(2,1)S(1)}, bf16[128,8192]{1,0:T(8,128)(2,1)}, u32[]{:S(2)}) copy-start(bf16[128,8192]{1,0:T(8,128)(2,1)} %all-gather.8.cloned.1.call-done) | copy-start | bytes 6291460
Sparse Core Ops, SparseCore 0:
  10.1 40.7 all-gather.3
  165.9 36.3 all-gather.5
  238.1 38.2 all-gather.7
where the time goes:
time: 301 us; the launch traced here: 300 us
  waiting for transfers between devices  98.9 us (33%)
  blocking collectives  77.6 us (26%)
  starting transfers between devices  55.3 us (18%)
  matrix products  32.2 us (11%)
  between operations  20.6 us (7%)
  other arithmetic  8.75 us (3%)
  local copies, waits for them, and re-layouts  6.07 us (2%)
    all_to_all x1, starting transfers between devices, per_device(): lax.all_to_all(slot_total, 'wide', split_axis=0, concat_axis=0, tiled=True)  48.1 us
    all_gather x1, waiting for transfers between devices, per_device(): piece = lax.all_gather(normed, 'wide', axis=1, tiled=True)  38.4 us
    all_gather x1, waiting for transfers between devices, per_device(): lax.all_gather(attended_rows, 'wide', axis=0, tiled=True)  35.7 us
    psum x1, blocking collectives, per_device(): squares = lax.psum(jnp.sum(branch * branch, axis=1), 'wide')  31.6 us
    all_gather x1, blocking collectives, per_device(): lax.all_gather(draft_keys, 'wide', axis=0, tiled=True)  23.9 us
    all_gather x1, blocking collectives, per_device(): lax.all_gather(draft_values, 'wide', axis=0, tiled=True)  22.1 us
    all_gather x1, waiting for transfers between devices, per_device(): lax.all_gather(queries, 'wide', axis=0, tiled=True)  9.54 us
    all_to_all x1, waiting for transfers between devices, per_device(): lax.all_to_all(slot_output, 'wide', split_axis=0, concat_axis=0, tiled=True)  9.29 us
  transfers between devices with their start and end apart: 6, of which 5 were waited for; matrix products, arithmetic and copies ran while one was open for 2% of the time, Pallas kernels for 0%

commit v1 on v0

--- a/solution.py
+++ b/solution.py
@@ -1,12 +1,18 @@
+import functools
 import math
 
 import jax
 import jax.numpy as jnp
 from jax import lax
+from jax.experimental import pallas as pl
+from jax.experimental.pallas import tpu as pltpu
 from jax.sharding import PartitionSpec as P
 
 very_low = -1e30
 epsilon = 1e-05
+tiles = 4
+chunk_rows = 1024
+weight_parts = 4
 
 
 def block_update(state, query_rows, block_keys, block_values, valid, scale):
@@ -53,7 +59,7 @@
     return block_update(state, query_rows, own_keys, own_values, own_valid[:, None, :], scale)
 
 
-def per_device(
+def plain_device(
     queries,
     draft_keys,
     draft_values,
@@ -170,6 +176,489 @@
     return (projected, hidden)
 
 
+def fused_kernel(
+    devices,
+    owner_ref,
+    lengths_ref,
+    packed_ref,
+    mask_ref,
+    gain_ref,
+    keys_hbm,
+    values_hbm,
+    out_hbm,
+    gate_hbm,
+    up_hbm,
+    projected_ref,
+    hidden_ref,
+    sent,
+    gathered,
+    query_all,
+    keys,
+    values,
+    outs,
+    stats,
+    attended,
+    branch,
+    gate_sum,
+    up_sum,
+    out_weight,
+    gate_weight,
+    up_weight,
+    local_sem,
+    direct_send,
+    direct_recv,
+    ring_send,
+    ring_recv,
+):
+    me = lax.axis_index("wide")
+    depth = devices // 4
+    place_z, place_y, place_c = me // 4, lax.rem(me // 2, 2), lax.rem(me, 2)
+    mirror_y = me + 2 - 4 * place_y
+    mirror_c = me + 1 - 2 * place_c
+    head_size = keys.shape[1]
+    key_heads = packed_ref.shape[0]
+    sequences, draft_rows = mask_ref.shape[0], mask_ref.shape[1]
+    senders = devices // sequences
+    local_rows = draft_rows // senders
+    group = query_all.shape[0] // draft_rows
+    blocks_per_pair = devices // (sequences * key_heads)
+    capacity = keys.shape[0]
+
+    def block_of(device):
+        block = jnp.int32(0)
+        for k in range(devices):
+            block = block + jnp.where(owner_ref[k] == device, jnp.int32(k), jnp.int32(0))
+        return jnp.minimum(block, devices - 1)
+
+    key_copy = pltpu.make_async_copy(keys_hbm, keys, local_sem.at[0])
+    value_copy = pltpu.make_async_copy(values_hbm, values, local_sem.at[1])
+    key_copy.start()
+    value_copy.start()
+
+    barrier = pltpu.get_barrier_semaphore()
+
+    def greet(k, carry):
+        pl.semaphore_signal(
+            barrier,
+            inc=1,
+            device_id={"wide": lax.rem(me + k, devices)},
+            device_id_type=pl.DeviceIdType.MESH,
+        )
+        return carry
+
+    lax.fori_loop(1, devices, greet, 0)
+
+    def fill(k, carry):
+        target = lax.rem(me + k, devices)
+        head = lax.rem(block_of(target) // blocks_per_pair, key_heads)
+        sent[target] = packed_ref[head]
+        return carry
+
+    lax.fori_loop(1, devices, fill, 0)
+    own_block = block_of(me)
+    own_pair = own_block // blocks_per_pair
+    own_sequence = own_pair // key_heads
+    own_head = lax.rem(own_pair, key_heads)
+    is_last = jnp.where(
+        lax.rem(own_block, blocks_per_pair) == blocks_per_pair - 1, jnp.int32(1), jnp.int32(0)
+    )
+    own_length = jnp.int32(0)
+    for k in range(devices):
+        own_length = own_length + jnp.where(owner_ref[k] == me, lengths_ref[k], jnp.int32(0))
+    gathered[me] = packed_ref[own_head]
+    pl.semaphore_wait(barrier, devices - 1)
+
+    def direct(target, source):
+        return pltpu.make_async_remote_copy(
+            src_ref=sent.at[target],
+            dst_ref=gathered.at[source],
+            send_sem=direct_send.at[target],
+            recv_sem=direct_recv.at[source],
+            device_id={"wide": target},
+            device_id_type=pl.DeviceIdType.MESH,
+        )
+
+    def send_direct(k, carry):
+        direct(lax.rem(me + k, devices), me).start()
+        return carry
+
+    lax.fori_loop(1, devices, send_direct, 0)
+
+    weight_copies = []
+    for number, (source, target) in enumerate(
+        ((out_hbm, out_weight), (gate_hbm, gate_weight), (up_hbm, up_weight))
+    ):
+        part = source.shape[0] // weight_parts
+        for piece in range(weight_parts):
+            rows = pl.ds(piece * part, part)
+            weight_copies.append(
+                pltpu.make_async_copy(
+                    source.at[rows],
+                    target.at[rows],
+                    local_sem.at[2 + number * weight_parts + piece],
+                )
+            )
+    for copy in weight_copies:
+        copy.start()
+
+    def wait_direct(k, carry):
+        other = lax.rem(me + k, devices)
+        descriptor = direct(other, other)
+        descriptor.wait_send()
+        descriptor.wait_recv()
+        return carry
+
+    lax.fori_loop(1, devices, wait_direct, 0)
+
+    def hop(item, direction, source, target):
+        buffer, phase = item
+        return pltpu.make_async_remote_copy(
+            src_ref=buffer.at[source],
+            dst_ref=buffer.at[source],
+            send_sem=ring_send.at[phase, direction, source],
+            recv_sem=ring_recv.at[phase, source],
+            device_id={"wide": target},
+            device_id_type=pl.DeviceIdType.MESH,
+        )
+
+    def launch(items, upward, downward, source, begin):
+        for item in items:
+            for use, step, direction in ((upward, 4, 0), (downward, -4, 1)):
+                if use:
+
+                    @pl.when((place_z + step // 4 >= 0) & (place_z + step // 4 < depth))
+                    def _(item=item, step=step, direction=direction):
+                        copy = hop(item, direction, source, me + step)
+                        copy.start() if begin else copy.wait_send()
+
+            copy = hop(item, 2, source, mirror_y)
+            copy.start() if begin else copy.wait_send()
+            copy = hop(item, 3, source, mirror_c)
+            copy.start() if begin else copy.wait_send()
+
+    def own_send(items, begin=True):
+        launch(items, True, True, me, begin)
+
+    def z_step(items, distance, begin=True):
+        @pl.when(place_z >= distance)
+        def _():
+            source = me - 4 * distance
+            if begin:
+                for item in items:
+                    hop(item, 0, source, me).wait_recv()
+            launch(items, True, False, source, begin)
+
+        @pl.when(place_z + distance < depth)
+        def _():
+            source = me + 4 * distance
+            if begin:
+                for item in items:
+                    hop(item, 1, source, me).wait_recv()
+            launch(items, False, True, source, begin)
+
+    def y_one(items, source, begin):
+        for item in items:
+            if begin:
+                hop(item, 2, source, me).wait_recv()
+            copy = hop(item, 3, source, mirror_c)
+            copy.start() if begin else copy.wait_send()
+
+    def y_step(items, distance, begin=True):
+        if distance == 0:
+            y_one(items, mirror_y, begin)
+        else:
+
+            @pl.when(place_z >= distance)
+            def _():
+                y_one(items, mirror_y - 4 * distance, begin)
+
+            @pl.when(place_z + distance < depth)
+            def _():
+                y_one(items, mirror_y + 4 * distance, begin)
+
+    def core_wait(items):
+        for half in range(devices // 2):
+            source = 2 * half + 1 - place_c
+            for item in items:
+                hop(item, 3, source, me).wait_recv()
+
+    def finish_sends(items):
+        own_send(items, False)
+        for distance in range(1, depth):
+            z_step(items, distance, False)
+        for distance in range(depth):
+            y_step(items, distance, False)
+
+    pieces = [
+        gathered[own_sequence * senders + number].astype(jnp.float32) for number in range(senders)
+    ]
+
+    def assembled(begin):
+        return jnp.concatenate(
+            [piece[begin : begin + local_rows] for piece in pieces], axis=0
+        ).astype(jnp.bfloat16)
+
+    for j in range(group):
+        query_all[j * draft_rows : (j + 1) * draft_rows] = assembled(j * local_rows)
+    draft_keys = assembled(group * local_rows)
+    draft_values = assembled((group + 1) * local_rows)
+    own_mask = mask_ref[own_sequence] * is_last
+
+    tile_heads = group // tiles
+    tile_rows = tile_heads * draft_rows
+    unit = math.log2(math.e) / math.sqrt(head_size)
+    steps = capacity // chunk_rows
+    lanes = lax.broadcasted_iota(jnp.int32, (draft_rows, stats.shape[2]), 1)
+    key_copy.wait()
+    value_copy.wait()
+
+    def update(state, scores, block_values):
+        peak, total, weighted = state
+        newest = jnp.maximum(peak, jnp.max(scores, axis=1, keepdims=True))
+        factor = jnp.exp2(peak - newest)
+        weights = jnp.exp2(scores - newest)
+        total = total * factor + jnp.sum(weights, axis=1, keepdims=True)
+        weighted = weighted * factor + jnp.dot(
+            weights.astype(jnp.bfloat16), block_values, preferred_element_type=jnp.float32
+        )
+        return newest, total, weighted
+
+    own_stats = jnp.zeros((draft_rows, stats.shape[2]), jnp.float32)
+    for tile in range(tiles):
+        query = query_all[tile * tile_rows : (tile + 1) * tile_rows]
+
+        def advance(number, state, query=query):
+            begin = pl.multiple_of(number * chunk_rows, chunk_rows)
+            scores = lax.dot_general(
+                query,
+                keys[pl.ds(begin, chunk_rows)],
+                (((1,), (1,)), ((), ())),
+                preferred_element_type=jnp.float32,
+            )
+            position = begin + lax.broadcasted_iota(jnp.int32, (1, chunk_rows), 1)
+            bias = jnp.where(position < own_length, 0.0, very_low)
+            return update(state, scores * unit + bias, values[pl.ds(begin, chunk_rows)])
+
+        state = (
+            jnp.full((tile_rows, 1), very_low, jnp.float32),
+            jnp.zeros((tile_rows, 1), jnp.float32),
+            jnp.zeros((tile_rows, head_size), jnp.float32),
+        )
+        cuts = [steps * cut // depth for cut in range(depth + 1)]
+        for cut in range(depth):
+            state = lax.fori_loop(cuts[cut], cuts[cut + 1], advance, state)
+            if tile > 0:
+                before = [(outs.at[tile - 1], tile - 1)]
+                if cut + 1 < depth:
+                    z_step(before, cut + 1)
+                else:
+                    for distance in range(depth):
+                        y_step(before, distance)
+        scores = lax.dot_general(
+            query, draft_keys, (((1,), (1,)), ((), ())), preferred_element_type=jnp.float32
+        )
+        visible = jnp.concatenate([own_mask] * tile_heads, axis=0) > 0
+        peak, total, weighted = update(
+            state, jnp.where(visible, scores * unit, very_low), draft_values
+        )
+        outs[tile, me] = (weighted / total).astype(jnp.bfloat16)
+        for k in range(tile_heads):
+            head = tile * tile_heads + k
+            rows = slice(k * draft_rows, (k + 1) * draft_rows)
+            own_stats = jnp.where(lanes == head, peak[rows], own_stats)
+            own_stats = jnp.where(lanes == group + head, total[rows], own_stats)
+        if tile + 1 == tiles:
+            stats[me] = own_stats
+            last = [(outs.at[tile], tile), (stats, tiles)]
+            own_send(last)
+        else:
+            own_send([(outs.at[tile], tile)])
+
+    for distance in range(1, depth):
+        z_step(last, distance)
+    for distance in range(depth):
+        y_step(last, distance)
+    core_wait([(outs.at[tile], tile) for tile in range(tiles)] + [(stats, tiles)])
+
+    for pair in range(sequences * key_heads):
+        owners = [owner_ref[pair * blocks_per_pair + b] for b in range(blocks_per_pair)]
+        each = [stats[owner] for owner in owners]
+        highest = functools.reduce(jnp.maximum, each)
+        mixing = [
+            jnp.exp2(one - highest) * pltpu.roll(one, one.shape[1] - group, 1) for one in each
+        ]
+        mixing_sum = functools.reduce(jnp.add, mixing)
+        shares = [one / mixing_sum for one in mixing]
+        top = pair // key_heads * draft_rows
+        for tile in range(tiles):
+            held = [outs[tile, owner].astype(jnp.float32) for owner in owners]
+            for k in range(tile_heads):
+                head = tile * tile_heads + k
+                rows = slice(k * draft_rows, (k + 1) * draft_rows)
+                mixed = functools.reduce(
+                    jnp.add,
+                    [share[:, head : head + 1] * one[rows] for share, one in zip(shares, held)],
+                )
+                left = (pair % key_heads * group + head) * head_size
+                attended[top : top + draft_rows, left : left + head_size] = mixed.astype(
+                    jnp.bfloat16
+                )
+
+    for copy in weight_copies[:weight_parts]:
+        copy.wait()
+    projected = jnp.dot(
+        attended[...], out_weight[...], preferred_element_type=jnp.float32
+    ).astype(jnp.bfloat16)
+    branch[me] = projected
+    phase = [(branch, tiles + 1)]
+    own_send(phase)
+    projected_ref[...] = projected
+    for copy in weight_copies[weight_parts:]:
+        copy.wait()
+
+    columns = branch.shape[2]
+    gate_sum[...] = jnp.zeros_like(gate_sum)
+    up_sum[...] = jnp.zeros_like(up_sum)
+
+    def absorb(source, squares):
+        part = branch[source].astype(jnp.float32)
+        scaled = (part * gain_ref[source]).astype(jnp.bfloat16)
+        rows = pl.ds(pl.multiple_of(source * columns, columns), columns)
+        gate_sum[...] += jnp.dot(scaled, gate_weight[rows], preferred_element_type=jnp.float32)
+        up_sum[...] += jnp.dot(scaled, up_weight[rows], preferred_element_type=jnp.float32)
+        return squares + jnp.sum(part * part, axis=1, keepdims=True)
+
+    squares = absorb(me, jnp.zeros((branch.shape[1], 1), jnp.float32))
+    z_step(phase, 1)
+    y_step(phase, 0)
+    squares = absorb(mirror_y, squares)
+    for distance in range(2, depth):
+        z_step(phase, distance)
+        y_step(phase, distance - 1)
+    y_step(phase, depth - 1)
+
+    def absorb_plane(k, total):
+        level = lax.rem(place_z + 1 + k // 2, depth)
+        return absorb(4 * level + 2 * lax.rem(k, 2) + place_c, total)
+
+    squares = lax.fori_loop(0, 2 * (depth - 1), absorb_plane, squares)
+
+    def absorb_other(k, total):
+        source = 2 * k + 1 - place_c
+        hop(phase[0], 3, source, me).wait_recv()
+        return absorb(source, total)
+
+    squares = lax.fori_loop(0, devices // 2, absorb_other, squares)
+    inverse = lax.rsqrt(squares / (columns * devices) + epsilon)
+    gate = gate_sum[...] * inverse
+    hidden_ref[...] = (gate / (1.0 + jnp.exp(-gate)) * (up_sum[...] * inverse)).astype(
+        jnp.bfloat16
+    )
+    finish_sends([(outs.at[tile], tile) for tile in range(tiles)] + [(stats, tiles)] + phase)
+
+
+def fused_device(
+    queries,
+    draft_keys,
+    draft_values,
+    cache_keys,
+    cache_values,
+    block_owner,
+    block_lengths,
+    draft_mask,
+    out_weight,
+    norm_gain,
+    gate_weight,
+    up_weight,
+):
+    devices = lax.axis_size("wide")
+    capacity, head_size = cache_keys.shape
+    key_heads = draft_keys.shape[1] // head_size
+    group = queries.shape[1] // head_size // key_heads
+    local_rows = queries.shape[0]
+    sequences, draft_rows = draft_mask.shape[:2]
+    rows = sequences * draft_rows
+    columns, units = out_weight.shape[1], gate_weight.shape[1]
+
+    def by_head(array, count):
+        parted = array.reshape(local_rows, key_heads, count, head_size)
+        return parted.transpose(1, 2, 0, 3).reshape(key_heads, count * local_rows, head_size)
+
+    packed = jnp.concatenate(
+        [by_head(queries, group), by_head(draft_keys, 1), by_head(draft_values, 1)], axis=1
+    )
+    vmem = pl.BlockSpec(memory_space=pltpu.VMEM)
+    smem = pl.BlockSpec(memory_space=pltpu.SMEM)
+    hbm = pl.BlockSpec(memory_space=pl.ANY)
+    half = jnp.bfloat16
+    return pl.pallas_call(
+        functools.partial(fused_kernel, devices),
+        out_shape=(
+            jax.ShapeDtypeStruct((rows, columns), half),
+            jax.ShapeDtypeStruct((rows, units), half),
+        ),
+        in_specs=[smem, smem, vmem, vmem, vmem, hbm, hbm, hbm, hbm, hbm],
+        out_specs=(vmem, vmem),
+        scratch_shapes=[
+            pltpu.VMEM((devices,) + packed.shape[1:], half),
+            pltpu.VMEM((devices,) + packed.shape[1:], half),
+            pltpu.VMEM((group * draft_rows, head_size), half),
+            pltpu.VMEM((capacity, head_size), half),
+            pltpu.VMEM((capacity, head_size), half),
+            pltpu.VMEM((tiles, devices, group // tiles * draft_rows, head_size), half),
+            pltpu.VMEM((devices, draft_rows, head_size), jnp.float32),
+            pltpu.VMEM((rows, out_weight.shape[0]), half),
+            pltpu.VMEM((devices, rows, columns), half),
+            pltpu.VMEM((rows, units), jnp.float32),
+            pltpu.VMEM((rows, units), jnp.float32),
+            pltpu.VMEM(out_weight.shape, half),
+            pltpu.VMEM(gate_weight.shape, half),
+            pltpu.VMEM(up_weight.shape, half),
+            pltpu.SemaphoreType.DMA((2 + 3 * weight_parts,)),
+            pltpu.SemaphoreType.DMA((devices,)),
+            pltpu.SemaphoreType.DMA((devices,)),
+            pltpu.SemaphoreType.DMA((tiles + 2, 4, devices)),
+            pltpu.SemaphoreType.DMA((tiles + 2, devices)),
+        ],
+        compiler_params=pltpu.CompilerParams(
+            collective_id=0, has_side_effects=True, vmem_limit_bytes=62 * 1024 * 1024
+        ),
+    )(
+        block_owner,
+        block_lengths,
+        packed,
+        draft_mask,
+        norm_gain.reshape(devices, 1, columns),
+        cache_keys,
+        cache_values,
+        out_weight,
+        gate_weight,
+        up_weight,
+    )
+
+
+def per_device(*arrays):
+    queries, cache_keys, draft_mask = arrays[0], arrays[3], arrays[7]
+    out_weight, gate_weight = arrays[8], arrays[10]
+    head_size = cache_keys.shape[1]
+    key_heads = arrays[1].shape[1] // head_size
+    group = queries.shape[1] // head_size // key_heads
+    whole_tiles = (
+        queries.shape[0] % 8 == 0
+        and lax.axis_size("wide") % 4 == 0
+        and draft_mask.shape[1] % 8 == 0
+        and head_size % 128 == 0
+        and 2 * group <= head_size
+        and group % tiles == 0
+        and out_weight.shape[1] % 128 == 0
+        and gate_weight.shape[1] % 128 == 0
+        and cache_keys.shape[0] % chunk_rows == 0
+        and out_weight.shape[0] % (16 * weight_parts) == 0
+        and gate_weight.shape[0] % (16 * weight_parts) == 0
+    )
+    return fused_device(*arrays) if whole_tiles else plain_device(*arrays)
+
+
 def solution(mesh):
     placed = (
         P(("grp", "wide"), None),

time: 301 us -> 110 us (0.37)
  Pallas kernels: 0 us -> 104 us
  waiting for transfers between devices: 98.9 us -> 0 us
  blocking collectives: 77.6 us -> 0 us
  starting transfers between devices: 55.3 us -> 0 us
  matrix products: 32.2 us -> 0 us
  between operations: 20.6 us -> 0.64 us
  other arithmetic: 8.75 us -> 1.52 us
    pallas_call x0 -> x1, Pallas kernels: none -> 104 us  [fused_device(): pl.pallas_call(functools.partial(fused_kernel, devices), out_shape=(jax.S...]
    all_gather x3 -> x0, waiting for transfers between devices: 83.7 us -> none  [the longest x1 38.4 us: per_device(): piece = lax.all_gather(normed, 'wide', axis=1, tiled=True)]
    all_to_all x3 -> x0, starting transfers between devices: 55.2 us -> none  [the longest x1 48.1 us: per_device(): lax.all_to_all(slot_total, 'wide', split_axis=0, concat_axis=0, tiled=True)]
    all_gather x2 -> x0, blocking collectives: 46 us -> none  [the longest x1 23.9 us: per_device(): lax.all_gather(draft_keys, 'wide', axis=0, tiled=True)]
    dot_general x14 -> x0, matrix products: 32.2 us -> none  [the longest x1 8.32 us: per_device(): upward = jnp.dot(piece, up_weight, preferred_element_type=jnp.float32)]
    psum x1 -> x0, blocking collectives: 31.6 us -> none  [per_device(): squares = lax.psum(jnp.sum(branch * branch, axis=1), 'wide')]
    all_to_all x3 -> x0, waiting for transfers between devices: 14.5 us -> none  [the longest x1 9.29 us: per_device(): lax.all_to_all(slot_output, 'wide', split_axis=0, concat_axis=0, tiled=True)]
  transfers between devices with their start and end apart: 6 -> 0, of which waited for: 5 -> 0; matrix products, arithmetic and copies ran while one was open for 2% -> 0% of each run, Pallas kernels for 0% -> 0%
where the time goes in v1:
time: 110 us
  Pallas kernels  104 us (95%)
  local copies, waits for them, and re-layouts  3.21 us (3%)
  other arithmetic  1.52 us (1%)
    pallas_call x1, Pallas kernels, fused_device(): pl.pallas_call(functools.partial(fused_kernel, devices), out_shape=(jax.S...  104 us
    unnamed x2, local copies, waits for them, and re-layouts  3.21 us

profile of v1, /device:TPU:0, one launch (start us, length us, event | category | flops | bytes accessed | tf_op | source)
XLA Modules:
  0.0 109.7 jit_solution(17842750782479024623)
XLA Ops:
  0.6 1.5 %pad_maximum_fusion.packed_ref = bf16[4,80,128]{2,1,0:T(8,128)(2,1)} fusion(bf16[4,8,128]{2,1,0:T(8,128)(2,1)} %bitcast.18, bf16[4,8,128]{2,1,0:T(8,128)(2,1)} %bitcast.19, bf16[4,64,128]{2,1,0:T(8,128)(2,1)} %bitcast.16), kind=kLoop, calls=%fused_computation | loop fusion | flops 245760 | bytes 163840 | tf_op jit(solution)/shard_map/concatenate | solution.py:587
  2.1 104.4 %shard_map.131 = (bf16[128,512]{1,0:T(8,128)(2,1)}, bf16[128,896]{1,0:T(8,128)(2,1)}) custom-call(s32[16]{0:T(128)} %owner_ref.1, s32[16]{0:T(128)} %lengths_ref.1, bf16[4,80,128]{2,1,0:T(8,128)(2,1)} %pad_maximum_fusion.packed_ref, s32[2,64,64]{2,1,0:T(8,128)} %mask_ref.1, f32[16,1,512]{2,1,0:T(1,128)} %bitcast.17, bf16[8192,128]{1,0:T(8,128)(2,1)} %keys_hbm.1, ...), custom_call_target="tpu_custom_call" | custom-call | tf_op jit(solution)/shard_map/pallas_call | solution.py:594
  106.5 1.6 %copy.16 = bf16[128,512]{1,0:T(8,128)(2,1)} copy(bf16[128,512]{1,0:T(8,128)(2,1)} %get-tuple-element.4) | data formatting | bytes 262144
  108.1 1.6 %copy.17 = bf16[128,896]{1,0:T(8,128)(2,1)} copy(bf16[128,896]{1,0:T(8,128)(2,1)} %get-tuple-element.5) | data formatting | bytes 458752

commit v2 on v1

--- a/solution.py
+++ b/solution.py
@@ -10,7 +10,7 @@
 
 very_low = -1e30
 epsilon = 1e-05
-tiles = 4
+tiles = 2
 chunk_rows = 1024
 weight_parts = 4
 
@@ -447,13 +447,8 @@
         cuts = [steps * cut // depth for cut in range(depth + 1)]
         for cut in range(depth):
             state = lax.fori_loop(cuts[cut], cuts[cut + 1], advance, state)
-            if tile > 0:
-                before = [(outs.at[tile - 1], tile - 1)]
-                if cut + 1 < depth:
-                    z_step(before, cut + 1)
-                else:
-                    for distance in range(depth):
-                        y_step(before, distance)
+            if tile > 0 and cut == depth // 2:
+                z_step([(outs.at[tile - 1], tile - 1)], 1)
         scores = lax.dot_general(
             query, draft_keys, (((1,), (1,)), ((), ())), preferred_element_type=jnp.float32
         )
@@ -474,10 +469,15 @@
         else:
             own_send([(outs.at[tile], tile)])
 
+    first = [(outs.at[tile], tile) for tile in range(tiles - 1)]
     for distance in range(1, depth):
+        if distance + 1 < depth:
+            z_step(first, distance + 1)
+        y_step(first, distance - 1)
         z_step(last, distance)
-    for distance in range(depth):
-        y_step(last, distance)
+        y_step(last, distance - 1)
+    y_step(first, depth - 1)
+    y_step(last, depth - 1)
     core_wait([(outs.at[tile], tile) for tile in range(tiles)] + [(stats, tiles)])
 
     for pair in range(sequences * key_heads):
@@ -535,20 +535,26 @@
     for distance in range(2, depth):
         z_step(phase, distance)
         y_step(phase, distance - 1)
+
+    def own_plane(row):
+        def body(k, total):
+            return absorb(4 * lax.rem(place_z + k, depth) + 2 * row + place_c, total)
+
+        return body
+
+    def other_plane(row):
+        def body(k, total):
+            source = 4 * lax.rem(place_z + k, depth) + 2 * row + 1 - place_c
+            hop(phase[0], 3, source, me).wait_recv()
+            return absorb(source, total)
+
+        return body
+
+    squares = lax.fori_loop(1, depth, own_plane(place_y), squares)
+    squares = lax.fori_loop(0, depth, other_plane(place_y), squares)
     y_step(phase, depth - 1)
-
-    def absorb_plane(k, total):
-        level = lax.rem(place_z + 1 + k // 2, depth)
-        return absorb(4 * level + 2 * lax.rem(k, 2) + place_c, total)
-
-    squares = lax.fori_loop(0, 2 * (depth - 1), absorb_plane, squares)
-
-    def absorb_other(k, total):
-        source = 2 * k + 1 - place_c
-        hop(phase[0], 3, source, me).wait_recv()
-        return absorb(source, total)
-
-    squares = lax.fori_loop(0, devices // 2, absorb_other, squares)
+    squares = lax.fori_loop(1, depth, own_plane(1 - place_y), squares)
+    squares = lax.fori_loop(0, depth, other_plane(1 - place_y), squares)
     inverse = lax.rsqrt(squares / (columns * devices) + epsilon)
     gate = gate_sum[...] * inverse
     hidden_ref[...] = (gate / (1.0 + jnp.exp(-gate)) * (up_sum[...] * inverse)).astype(

time: 110 us -> 77 us (0.70)
  Pallas kernels: 104 us -> 71.4 us
    pallas_call x1, Pallas kernels: 104 us -> 71.4 us  [fused_device(): pl.pallas_call(functools.partial(fused_kernel, devices), out_shape=(jax.S...]
where the time goes in v2:
time: 77 us; the launch traced here: 76.8 us
  Pallas kernels  71.4 us (93%)
  local copies, waits for them, and re-layouts  3.21 us (4%)
  other arithmetic  1.52 us (2%)
    pallas_call x1, Pallas kernels, fused_device(): pl.pallas_call(functools.partial(fused_kernel, devices), out_shape=(jax.S...  71.4 us
    unnamed x2, local copies, waits for them, and re-layouts  3.21 us

profile of v2, /device:TPU:0, one launch (start us, length us, event | category | flops | bytes accessed | tf_op | source)
XLA Modules:
  0.0 76.8 jit_solution(14383843656218875034)
XLA Ops:
  0.6 1.5 %pad_maximum_fusion.packed_ref = bf16[4,80,128]{2,1,0:T(8,128)(2,1)} fusion(bf16[4,8,128]{2,1,0:T(8,128)(2,1)} %bitcast.18, bf16[4,8,128]{2,1,0:T(8,128)(2,1)} %bitcast.19, bf16[4,64,128]{2,1,0:T(8,128)(2,1)} %bitcast.16), kind=kLoop, calls=%fused_computation | loop fusion | flops 245760 | bytes 163840 | tf_op jit(solution)/shard_map/concatenate | solution.py:593
  2.1 71.4 %shard_map.131 = (bf16[128,512]{1,0:T(8,128)(2,1)}, bf16[128,896]{1,0:T(8,128)(2,1)}) custom-call(s32[16]{0:T(128)} %owner_ref.1, s32[16]{0:T(128)} %lengths_ref.1, bf16[4,80,128]{2,1,0:T(8,128)(2,1)} %pad_maximum_fusion.packed_ref, s32[2,64,64]{2,1,0:T(8,128)} %mask_ref.1, f32[16,1,512]{2,1,0:T(1,128)} %bitcast.17, bf16[8192,128]{1,0:T(8,128)(2,1)} %keys_hbm.1, ...), custom_call_target="tpu_custom_call" | custom-call | tf_op jit(solution)/shard_map/pallas_call | solution.py:600
  73.6 1.6 %copy.16 = bf16[128,512]{1,0:T(8,128)(2,1)} copy(bf16[128,512]{1,0:T(8,128)(2,1)} %get-tuple-element.4) | data formatting | bytes 262144
  75.1 1.6 %copy.17 = bf16[128,896]{1,0:T(8,128)(2,1)} copy(bf16[128,896]{1,0:T(8,128)(2,1)} %get-tuple-element.5) | data formatting | bytes 458752
